TPU v7x, 128 devices: a whole 4x4x4 slice. The times are simulated.
128 devices in a mesh: row: 8 (over x, z_lo), col: 16 (over z_hi, y, core).
Axes of the slice: x: 4, y: 4, z: 4 (z_hi: 2, z_lo: 2; z = z_hi * 2 + z_lo), core: 2. Of those that a mesh axis runs over, the one named last changes fastest.
Arguments:
- a_cols: bfloat16 [16384, 8192], P('row', 'col'), may hold values from -6 to 6
- owners: int32 [1024], replicated, may hold values from 0 to 15
- column_slot: int32 [1024], replicated, may hold values from 0 to 511
- update_flag: int32 [1024], replicated, may hold values from 0 to 1
- rescale: float32 [1024], replicated, may hold values from 0.5 to 2
- inverses: bfloat16 [2, 512, 512], replicated, may hold values from -0.0078125 to 0.0078125
- trailing: float32 [16384, 16384], P('row', 'col'), may hold values from -0.15625 to 0.15625
Outputs:
- updated_slab: float32 [16384, 16384], P('row', 'col')
- panels: bfloat16 [16384, 1024], P('row')
All inputs are finite; a program needn't handle non-finite values.
Results may differ from a plain program's by a relative error of at most 0.013.
The roundings to bfloat16 on the way count: a program that leaves them out, or rounds other values in their place, can miss the bound.
Values may be sent and summed in bfloat16 or wider, within the bound.
No kernel may reach another device: no remote copies, remote signals or barrier semaphores. Data moves between devices by JAX's collectives and lax.ppermute only.
A program may use at most 128 MiB of HBM per device.

v0:
```python
import jax
import jax.numpy as jnp
from jax import lax
from jax.sharding import PartitionSpec as P


def from_root(value, axis, source):
    kept = jnp.where(lax.axis_index(axis) == source, value, 0).astype(value.dtype)
    return lax.psum(kept, axis)


def panel_pass(columns, inverses, signed, reducer):
    width = inverses.shape[1]
    first_cols = columns[:, :width]
    second_cols = columns[:, width:]
    first_panel = jnp.dot(first_cols, inverses[0], preferred_element_type=jnp.float32).astype(
        jnp.bfloat16
    )
    gram_block = reducer(
        lax.dot_general(
            first_panel, second_cols, (((0,), (0,)), ((), ())), preferred_element_type=jnp.float32
        )
    )
    weighted = first_panel * signed[:width][None, :]
    coupled = (
        second_cols.astype(jnp.float32)
        - jnp.dot(weighted, gram_block.astype(jnp.bfloat16), preferred_element_type=jnp.float32)
    ).astype(jnp.bfloat16)
    second_panel = jnp.dot(coupled, inverses[1], preferred_element_type=jnp.float32).astype(
        jnp.bfloat16
    )
    return jnp.concatenate([first_panel, second_panel], axis=1)


def body(a_cols, owners, column_slot, update_flag, rescale, inverses, trailing):
    column_index = lax.axis_index("col")
    picked = jnp.take(a_cols, column_slot, axis=1)
    owned = owners == column_index
    partial_cols = jnp.where(owned[None, :], picked, jnp.zeros((), jnp.bfloat16))
    signed = (2 * update_flag - 1).astype(jnp.bfloat16)
    summed = lax.psum(partial_cols, "col").astype(jnp.float32)
    columns = (summed * rescale[None, :]).astype(jnp.bfloat16)
    panels = panel_pass(columns, inverses, signed, lambda matrix: lax.psum(matrix, "row"))
    block_rows = panels.shape[0]
    block_cols = trailing.shape[1]
    source = column_index * block_cols // block_rows
    offset = column_index * block_cols % block_rows
    strip_rows = lax.dynamic_slice_in_dim(panels, offset, block_cols, 0)
    column_panels = from_root(strip_rows, "row", source)
    weighted = panels * signed[None, :]
    update = lax.dot_general(
        weighted, column_panels, (((1,), (1,)), ((), ())), preferred_element_type=jnp.float32
    )
    return (trailing + update, panels)


def solution(mesh):
    placed = (P("row", "col"), P(), P(), P(), P(), P(), P("row", "col"))
    return jax.shard_map(
        body,
        mesh=mesh,
        in_specs=placed,
        out_specs=(P("row", "col"), P("row", None)),
        check_vma=False,
    )
```

profile of v0, /device:TPU:8, one launch (start us, length us, event | category | flops | bytes accessed | tf_op | source)
XLA Modules:
  0.0 379.0 jit_solution(7499403749165712552)
XLA Ops:
  7.2 0.0 copy-start.1
  7.2 0.0 copy-start.6
  7.2 0.0 all-reduce.4.cloned.1.call-start
  7.2 2.9 copy.9
  10.2 0.0 copy-done.1
  10.2 0.0 copy-done.6
  10.2 6.0 %gather_fusion = bf16[1024,2048]{1,0:T(8,128)(2,1)} fusion(bf16[2048,512]{0,1:T(8,128)(2,1)S(1)} %copy.9, s32[1024]{0:T(1024)S(1)} %fusion.22), kind=kCustom, calls=%fused_computation | custom fusion | bytes 8392704 | tf_op jit(solution)/shard_map/jit(_take)/gather | solution.py:37
  16.2 4.1 %select_bitcast_fusion = bf16[2048,1024]{0,1:T(8,128)(2,1)} fusion(bf16[1024,2048]{1,0:T(8,128)(2,1)} %gather_fusion, pred[1024]{0:T(1024)(128)(4,1)S(1)} %get-tuple-element.5, pred[1024]{0:T(1024)(128)(4,1)S(1)} %get-tuple-element.4), kind=kLoop, calls=%fused_computation.5 | loop fusion | flops 4194304 | bytes 8390656 | tf_op jit(solution)/shard_map/jit(_where)/select_n | solution.py:39
  20.3 0.0 copy-start.5
  20.3 0.0 copy-start.4
  20.3 0.0 all-reduce.4.cloned.1.call-update
  20.3 0.0 all-reduce.6.cloned.1.call-start
  20.4 0.6 copy-done.5
  21.0 0.0 copy-start.2
  21.0 0.0 copy-start.7
  21.0 147.4 %all-reduce.4.cloned.1.call-done = bf16[2048,1024]{0,1:T(8,128)(2,1)} async-done(((bf16[2048,1024]{0,1:T(8,128)(2,1)}), bf16[2048,1024]{0,1:T(8,128)(2,1)}) %all-reduce.4.cloned.1.call-update) | async-done | bytes 4194320 | tf_op jit(solution)/shard_map/psum | solution.py:41
  168.4 0.0 copy-done.4
  168.4 2.9 multiply_convert_fusion
  171.3 0.0 copy-done.2
  171.3 0.0 copy-done.7
  171.3 0.0 copy-start
  171.3 1.3 convolution_convert_fusion.1
  172.7 0.7 copy-done
  173.3 0.0 slice-start
  173.3 1.3 fusion.10
  174.6 69.1 %all-reduce.7 = bf16[512,512]{1,0:T(8,128)(2,1)} all-reduce(f32[512,512]{1,0:T(8,128)S(1)} %fusion.10), channel_id=1, replica_groups=mesh['row'=8,'col'=16] {'row'}, use_global_device_ids=true, to_apply=%region_1.2 | all-reduce | flops 262144 | bytes 1572864 | tf_op jit(solution)/shard_map/psum | solution.py:43
  243.7 0.0 slice-done
  243.7 5.7 %convolution_convert_fusion = bf16[2048,512]{0,1:T(8,128)(2,1)} fusion(bf16[2048,512]{0,1:T(8,128)(2,1)S(1)} %convolution_convert_fusion.1, bf16[2048,1024]{0,1:T(8,128)(2,1)} %copy-done, bf16[512]{0:T(512)(128)(2,1)S(1)} %slice-done, bf16[2,512,512]{2,1,0:T(8,128)(2,1)} %param.12, bf16[512,512]{1,0:T(8,128)(2,1)} %all-reduce.7), kind=kOutput, calls=%fused_computation.10 | convolution fusion | flops 2152726528 | bytes 7341056 | tf_op jit(solution)/shard_map/dot_general | solution.py:29
  249.4 3.1 fusion.6
  252.5 0.0 all-reduce.6.cloned.1.call-update
  252.5 4.2 %pad_maximum_fusion = bf16[2048,1024]{0,1:T(8,128)(2,1)} fusion(bf16[2048,512]{0,1:T(8,128)(2,1)} %convolution_convert_fusion, bf16[2048,512]{0,1:T(8,128)(2,1)S(1)} %convolution_convert_fusion.1), kind=kLoop, calls=%fused_computation.3 | loop fusion | flops 8388608 | bytes 8388608 | tf_op jit(solution)/shard_map/concatenate | solution.py:32
  256.7 0.0 copy-start.3
  256.7 6.4 %copy.10 = bf16[2048,1024]{1,0:T(8,128)(2,1)} copy(bf16[2048,1024]{0,1:T(8,128)(2,1)} %pad_maximum_fusion) | data formatting | bytes 8388608
  263.1 96.3 %all-reduce.6.cloned.1.call-done = bf16[1024,1024]{0,1:T(8,128)(2,1)} async-done(((bf16[1024,1024]{0,1:T(8,128)(2,1)}), bf16[1024,1024]{0,1:T(8,128)(2,1)}) %all-reduce.6.cloned.1.call-update) | async-done | bytes 2097168 | tf_op jit(solution)/shard_map/psum | solution.py:9
  359.4 0.0 copy-done.3
  359.4 12.8 %fusion.2 = f32[2048,1024]{1,0:T(8,128)} fusion(f32[2048,1024]{1,0:T(8,128)} %param.13, bf16[1024,1024]{0,1:T(8,128)(2,1)} %all-reduce.6.cloned.1.call-done, bf16[1024]{0:T(1024)(128)(2,1)S(1)} %copy-done.3, bf16[2048,512]{0,1:T(8,128)(2,1)} %convolution_convert_fusion, bf16[2048,512]{0,1:T(8,128)(2,1)S(1)} %convolution_convert_fusion.1), kind=kOutput, calls=%fused_computation.9 | convolution fusion | flops 4309647360 | bytes 23070720 | tf_op jit(solution)/shard_map/dot_general | solution.py:51
  (3 shorter events, 0.0 us)
Async XLA Ops:
  7.2 3.0 copy-start.1
  7.2 3.0 copy-start.6
  7.2 161.2 %all-reduce.4.cloned.1.call-start = ((), (), s32[]{:S(2)}) async-start(), calls=%async_computation | async-start | bytes 8388608 | tf_op jit(solution)/shard_map/psum | solution.py:41
  20.3 0.7 copy-start.5
  20.3 148.1 %copy-start.4 = (f32[1024]{0:T(1024)S(1)}, f32[1024]{0:T(1024)}, u32[]{:S(2)}) copy-start(f32[1024]{0:T(1024)} %param.11) | copy-start | bytes 12292
  20.3 339.1 %all-reduce.6.cloned.1.call-start = ((), (), s32[]{:S(2)}) async-start(), calls=%async_computation.1 | async-start | bytes 4194304 | tf_op jit(solution)/shard_map/psum | solution.py:9
  21.0 150.3 %copy-start.2 = (bf16[1024]{0:T(1024)(128)(2,1)}, bf16[1024]{0:T(1024)(128)(2,1)S(1)}, u32[]{:S(2)}) copy-start(bf16[1024]{0:T(1024)(128)(2,1)S(1)} %add_convert_fusion) | copy-start | bytes 6148
  21.0 150.3 %copy-start.7 = (bf16[2,512,512]{2,1,0:T(8,128)(2,1)S(1)}, bf16[2,512,512]{2,1,0:T(8,128)(2,1)}, u32[]{:S(2)}) copy-start(bf16[2,512,512]{2,1,0:T(8,128)(2,1)} %param.12) | copy-start | bytes 3145732
  171.3 2.0 copy-start
  173.3 70.4 %slice-start = ((bf16[1024]{0:T(1024)(128)(2,1)}), bf16[512]{0:T(512)(128)(2,1)S(1)}, s32[]{:S(2)}) async-start(bf16[1024]{0:T(1024)(128)(2,1)} %copy-done.2), calls=%async_computation.2 | async-start | bytes 2048 | tf_op jit(solution)/shard_map/slice | solution.py:24
  256.7 102.7 %copy-start.3 = (bf16[1024]{0:T(1024)(128)(2,1)S(1)}, bf16[1024]{0:T(1024)(128)(2,1)}, u32[]{:S(2)}) copy-start(bf16[1024]{0:T(1024)(128)(2,1)} %copy-done.2) | copy-start | bytes 6148
Sparse Core Ops, SparseCore 0:
  20.4 147.8 all-reduce.3
  252.6 106.7 all-reduce.5
where the time goes:
time: 380 us; the launch traced here: 379 us
  waiting for transfers between devices  244 us (64%)
  blocking collectives  69.1 us (18%)
  matrix products  21.1 us (6%)
  local copies, waits for them, and re-layouts  16.6 us (4%)
  other arithmetic  14.3 us (4%)
  between operations  14.2 us (4%)
    psum x1, waiting for transfers between devices, body(): summed = lax.psum(partial_cols, 'col').astype(jnp.float32)  147 us
    psum x1, waiting for transfers between devices, from_root(): return lax.psum(kept, axis)  96.3 us
    psum x1, blocking collectives, body(): lax.psum(matrix, 'row')  69.1 us
    dot_general x1, matrix products, body(): lax.dot_general(weighted, column_panels, (((1,), (1,)), ((), ())), prefer...  12.8 us
    unnamed x18, local copies, waits for them, and re-layouts  10.6 us
  transfers between devices with their start and end apart: 2, of which 2 were waited for; matrix products, arithmetic and copies ran while one was open for 3% of the time, Pallas kernels for 0%

commit v1 on v0

--- a/solution.py
+++ b/solution.py
@@ -33,6 +33,11 @@
 
 
 def body(a_cols, owners, column_slot, update_flag, rescale, inverses, trailing):
+
+    def _balance_tasks(state, bus_axis):
+        latest = lax.all_gather(state, bus_axis)
+        return jnp.sum(latest, axis=0)
+
     column_index = lax.axis_index("col")
     picked = jnp.take(a_cols, column_slot, axis=1)
     owned = owners == column_index
@@ -40,7 +45,7 @@
     signed = (2 * update_flag - 1).astype(jnp.bfloat16)
     summed = lax.psum(partial_cols, "col").astype(jnp.float32)
     columns = (summed * rescale[None, :]).astype(jnp.bfloat16)
-    panels = panel_pass(columns, inverses, signed, lambda matrix: lax.psum(matrix, "row"))
+    panels = panel_pass(columns, inverses, signed, lambda matrix: _balance_tasks(matrix, "row"))
     block_rows = panels.shape[0]
     block_cols = trailing.shape[1]
     source = column_index * block_cols // block_rows

time: 380 us -> 491 us (1.29)
  waiting for transfers between devices: 244 us -> 419 us
  blocking collectives: 69.1 us -> 0 us
    all_gather x0 -> x1, waiting for transfers between devices: none -> 174 us  [_balance_tasks(): latest = lax.all_gather(state, bus_axis)]
    psum x1 -> x0, blocking collectives: 69.1 us -> none  [body(): lax.psum(matrix, 'row')]
    unnamed x18 -> x14, local copies, waits for them, and re-layouts: 10.6 us -> 10 us
  transfers between devices with their start and end apart: 2 -> 3, of which waited for: 2 -> 3; matrix products, arithmetic and copies ran while one was open for 3% -> 2% of each run, Pallas kernels for 0% -> 0%
where the time goes in v1:
time: 491 us; the launch traced here: 490 us
  waiting for transfers between devices  419 us (85%)
  matrix products  21.9 us (4%)
  other arithmetic  18.8 us (4%)
  local copies, waits for them, and re-layouts  16 us (3%)
  between operations  13.9 us (3%)
    all_gather x1, waiting for transfers between devices, _balance_tasks(): latest = lax.all_gather(state, bus_axis)  174 us
    psum x1, waiting for transfers between devices, body(): summed = lax.psum(partial_cols, 'col').astype(jnp.float32)  148 us
    psum x1, waiting for transfers between devices, from_root(): return lax.psum(kept, axis)  97.1 us
    dot_general x1, matrix products, body(): lax.dot_general(weighted, column_panels, (((1,), (1,)), ((), ())), prefer...  12.8 us
    unnamed x14, local copies, waits for them, and re-layouts  10 us
  transfers between devices with their start and end apart: 3, of which 3 were waited for; matrix products, arithmetic and copies ran while one was open for 2% of the time, Pallas kernels for 0%

profile of v1, /device:TPU:8, one launch (start us, length us, event | category | flops | bytes accessed | tf_op | source)
XLA Modules:
  0.0 490.1 jit_solution(4044500137306189386)
XLA Ops:
  7.2 0.0 copy-start.1
  7.2 0.0 copy-start.4
  7.2 0.0 all-reduce.3.cloned.1.call-start
  7.2 2.9 copy.9
  10.2 0.0 copy-done.1
  10.2 0.0 copy-done.4
  10.2 6.0 %gather_fusion = bf16[1024,2048]{1,0:T(8,128)(2,1)} fusion(bf16[2048,512]{0,1:T(8,128)(2,1)S(1)} %copy.9, s32[1024]{0:T(1024)S(1)} %fusion.22), kind=kCustom, calls=%fused_computation | custom fusion | bytes 8392704 | tf_op jit(solution)/shard_map/jit(_take)/gather | solution.py:42
  16.2 4.1 select_bitcast_fusion
  20.3 0.0 copy-start.2
  20.3 0.0 all-reduce.3.cloned.1.call-update
  20.3 0.0 copy-start.5
  20.3 0.0 all-gather.3.cloned.1.call-start
  20.4 148.0 %all-reduce.3.cloned.1.call-done = bf16[2048,1024]{0,1:T(8,128)(2,1)} async-done(((bf16[2048,1024]{0,1:T(8,128)(2,1)}), bf16[2048,1024]{0,1:T(8,128)(2,1)}) %all-reduce.3.cloned.1.call-update) | async-done | bytes 4194320 | tf_op jit(solution)/shard_map/psum | solution.py:46
  168.4 0.0 copy-done.2
  168.4 2.9 multiply_convert_fusion
  171.3 0.0 copy-done.5
  171.3 0.0 copy-start
  171.3 1.3 convolution_convert_fusion.1
  172.6 0.7 copy-done
  173.3 0.0 copy-start.3
  173.3 2.3 fusion.10
  175.6 0.0 all-gather.3.cloned.1.call-update
  175.6 0.2 all-reduce.5.cloned.1.call-start
  175.9 0.0 copy-done.3
  175.9 174.1 %all-gather.3.cloned.1.call-done = f32[4096,512]{1,0:T(8,128)} async-done(((f32[512,512]{1,0:T(8,128)}), f32[4096,512]{1,0:T(8,128)}) %all-gather.3.cloned.1.call-update) | async-done | bytes 8388624 | tf_op jit(solution)/shard_map/all_gather | solution.py:38
  350.0 4.4 reduce_sum.9
  354.4 5.6 %convolution_convert_fusion = bf16[2048,512]{0,1:T(8,128)(2,1)} fusion(bf16[2048,512]{0,1:T(8,128)(2,1)S(1)} %convolution_convert_fusion.1, bf16[2048,1024]{0,1:T(8,128)(2,1)} %copy-done, bf16[512]{0:T(512)(128)(2,1)S(1)} %slice.18, bf16[2,512,512]{2,1,0:T(8,128)(2,1)} %param.12, bf16[512,512]{1,0:T(8,128)(2,1)S(1)} %reduce_sum.9), kind=kOutput, calls=%fused_computation.10 | convolution fusion | flops 2152726528 | bytes 7341056 | tf_op jit(solution)/shard_map/dot_general | solution.py:29
  360.0 3.1 fusion.6
  363.1 0.0 all-reduce.5.cloned.1.call-update
  363.1 4.2 pad_maximum_fusion
  367.3 6.4 %copy.10 = bf16[2048,1024]{1,0:T(8,128)(2,1)} copy(bf16[2048,1024]{0,1:T(8,128)(2,1)} %pad_maximum_fusion) | data formatting | bytes 8388608
  373.7 97.1 %all-reduce.5.cloned.1.call-done = bf16[1024,1024]{0,1:T(8,128)(2,1)} async-done(((bf16[1024,1024]{0,1:T(8,128)(2,1)}), bf16[1024,1024]{0,1:T(8,128)(2,1)}) %all-reduce.5.cloned.1.call-update) | async-done | bytes 2097168 | tf_op jit(solution)/shard_map/psum | solution.py:9
  470.8 12.8 %fusion.2 = f32[2048,1024]{1,0:T(8,128)} fusion(f32[2048,1024]{1,0:T(8,128)} %param.13, bf16[1024,1024]{0,1:T(8,128)(2,1)} %all-reduce.5.cloned.1.call-done, bf16[1024]{0:T(1024)(128)(2,1)S(1)} %add_convert_fusion, bf16[2048,512]{0,1:T(8,128)(2,1)} %convolution_convert_fusion, bf16[2048,512]{0,1:T(8,128)(2,1)S(1)} %convolution_convert_fusion.1), kind=kOutput, calls=%fused_computation.9 | convolution fusion | flops 4309647360 | bytes 23070720 | tf_op jit(solution)/shard_map/dot_general | solution.py:56
  (4 shorter events, 0.0 us)
Async XLA Ops:
  7.2 3.0 copy-start.1
  7.2 3.0 copy-start.4
  7.2 161.2 %all-reduce.3.cloned.1.call-start = ((), (), s32[]{:S(2)}) async-start(), calls=%async_computation | async-start | bytes 8388608 | tf_op jit(solution)/shard_map/psum | solution.py:46
  20.3 148.1 %copy-start.2 = (f32[1024]{0:T(1024)S(1)}, f32[1024]{0:T(1024)}, u32[]{:S(2)}) copy-start(f32[1024]{0:T(1024)} %param.11) | copy-start | bytes 12292
  20.3 151.0 %copy-start.5 = (bf16[2,512,512]{2,1,0:T(8,128)(2,1)S(1)}, bf16[2,512,512]{2,1,0:T(8,128)(2,1)}, u32[]{:S(2)}) copy-start(bf16[2,512,512]{2,1,0:T(8,128)(2,1)} %param.12) | copy-start | bytes 3145732
  20.3 329.7 %all-gather.3.cloned.1.call-start = ((), (), s32[]{:S(2)}) async-start(), calls=%async_computation.2 | async-start | bytes 9437184 | tf_op jit(solution)/shard_map/all_gather | solution.py:38
  171.3 2.0 copy-start
  173.3 2.5 copy-start.3
  175.6 295.2 %all-reduce.5.cloned.1.call-start = ((), (), s32[]{:S(2)}) async-start(), calls=%async_computation.1 | async-start | bytes 4194304 | tf_op jit(solution)/shard_map/psum | solution.py:9
Sparse Core Ops, SparseCore 0:
  20.4 147.8 all-reduce.2
  175.7 174.2 all-gather.2
  363.2 107.4 all-reduce.4
